TPU v7x, 1024 devices: a whole 4x4x32 slice. The times are simulated.
1024 devices in a mesh: section: 16 (over y, x), expert: 64 (over z, core).
Axes of the slice: x: 4, y: 4, z: 32, core: 2. Of those that a mesh axis runs over, the one named last changes fastest.
Arguments:
- forward_sent: bfloat16 [16, 4096, 2048], P('section', 'expert'), may hold values from -6 to 6
- embedded: bfloat16 [4096, 2048], P('expert'), may hold values from -6 to 6
- forward_routes: int32 [16, 4096, 2], P('section', 'expert'), may hold values from 0 to 63, all different within a row; in each aligned block of 64 rows (0 to 63, 64 to 127, ..., all dimensions but the last counted through in order) at most 3 rows name the same one
- backward_sent: bfloat16 [16, 4096, 2048], P('section', 'expert'), may hold values from -6 to 6
- loss_gradient: bfloat16 [4096, 2048], P('expert'), may hold values from -6 to 6
- saved_inputs: bfloat16 [16, 4096, 2048], P('section', 'expert'), may hold values from -6 to 6
- backward_routes: int32 [16, 4096, 2], P('section', 'expert'), may hold values from 0 to 63, all different within a row; in each aligned block of 64 rows (0 to 63, 64 to 127, ..., all dimensions but the last counted through in order) at most 3 rows name the same one
- pre_activation: bfloat16 [16, 64, 64, 3, 1024], P('section', None, 'expert'), may hold values from -6 to 6
- norm_gain: bfloat16 [16, 2048], P('section'), may hold values from 0.099609375 to 1.8984375
- router: bfloat16 [16, 2048, 64], P('section'), may hold values from -0.125 to 0.125
- up_weight: bfloat16 [64, 2048, 1024], P('expert'), may hold values from -0.125 to 0.125
- down_weight: bfloat16 [64, 1024, 2048], P('expert'), may hold values from -0.1875 to 0.1875
Outputs:
- forward_output: bfloat16 [16, 4096, 2048], P('section', 'expert')
- input_gradient: bfloat16 [16, 4096, 2048], P('section', 'expert')
Inputs may be any that keep to these rules, and one draw needn't show every extreme that they name: `forward_routes`: in each aligned block of 64 rows (one device's tokens at one section) no expert is named by more than 3 rows, a bound that some block reaches; the 2 entries of a row differ. `backward_routes`: in each aligned block of 64 rows (one device's tokens at one section) no expert is named by more than 3 rows, a bound that some block reaches; the 2 entries of a row differ.
All inputs are finite; a program needn't handle non-finite values.
Results may differ from a plain program's by a relative error of at most 0.0053.
Values may be sent and summed in bfloat16 or wider, within the bound.
A program may use at most 32 MiB of HBM per device.

v0:
```python
import jax
import jax.numpy as jnp
from jax import lax
from jax.sharding import PartitionSpec as P

EPS = 1e-06
HIGH = lax.Precision.HIGHEST


def from_behind(block, axis, distance):
    devices = range(lax.axis_size(axis))
    route = [(i - distance, i) for i in devices if i - distance in devices]
    return lax.ppermute(block, axis, route)


def slot_targets(routes, experts, capacity):
    flattened = routes.reshape(-1)
    onehot = (flattened[:, None] == jnp.arange(experts, dtype=jnp.int32)[None, :]).astype(jnp.int32)
    before = jnp.cumsum(onehot, axis=0) - onehot
    ranked = jnp.sum(before * onehot, axis=1)
    return (flattened * capacity + ranked).reshape(routes.shape)


def prepare_routes(tokens, gain_row, router_mat, routes, experts, capacity):
    widened = tokens.astype(jnp.float32)
    inv_rms = lax.rsqrt(jnp.mean(widened * widened, axis=-1) + EPS)
    normed = (widened * inv_rms[:, None] * gain_row.astype(jnp.float32)).astype(jnp.bfloat16)
    logits = jnp.dot(normed, router_mat, preferred_element_type=jnp.float32)
    chosen = jnp.take_along_axis(logits, routes, axis=1)
    exponent = jnp.exp(chosen)
    shares = exponent / jnp.sum(exponent, axis=1, keepdims=True)
    rounded = lax.optimization_barrier(shares.astype(jnp.bfloat16)).astype(jnp.float32)
    targets = slot_targets(routes, experts, capacity)
    slot_table = (targets[..., None] == jnp.arange(experts * capacity, dtype=jnp.int32)).astype(
        jnp.float32
    )
    placing = jnp.sum(slot_table, axis=1).astype(jnp.bfloat16)
    mixing = jnp.sum(slot_table * rounded[..., None], axis=1).astype(jnp.bfloat16)
    return (widened, inv_rms, normed, shares, slot_table, placing, mixing)


def on_device(
    forward_sent,
    embedded,
    forward_routes,
    backward_sent,
    loss_gradient,
    saved_inputs,
    backward_routes,
    pre_activation,
    norm_gain,
    router,
    up_weight,
    down_weight,
):
    section_index = lax.axis_index("section")
    final_section = lax.axis_size("section") - 1
    sources = lax.axis_size("expert")
    experts = router.shape[2]
    capacity = pre_activation.shape[3]
    local_count = up_weight.shape[0]
    width = up_weight.shape[1]
    slots = experts * capacity
    gain_row = norm_gain[0]
    router_mat = router[0]
    arrived = from_behind(forward_sent[0], "section", 1)
    tokens = jnp.where(section_index == 0, embedded, arrived)
    returned_grad = from_behind(backward_sent[0], "section", -1)
    upstream = jnp.where(section_index == final_section, loss_gradient, returned_grad)
    widened, inv_rms, normed, shares, slot_table, placing, mixing = prepare_routes(
        tokens, gain_row, router_mat, forward_routes[0], experts, capacity
    )
    saved_wide, saved_rms, saved_normed, saved_shares, saved_table, saved_placing, saved_mixing = (
        prepare_routes(saved_inputs[0], gain_row, router_mat, backward_routes[0], experts, capacity)
    )
    send_forward = jnp.einsum(
        "ts,td->sd", placing, normed, preferred_element_type=jnp.float32
    ).astype(jnp.bfloat16)
    send_forward = send_forward.reshape(sources, local_count * capacity, width)
    send_backward = jnp.einsum(
        "ts,td->sd", saved_placing, upstream, preferred_element_type=jnp.float32
    ).astype(jnp.bfloat16)
    send_backward = send_backward.reshape(sources, local_count * capacity, width)
    saved_pre = pre_activation[0].astype(jnp.float32)
    got_forward = lax.all_to_all(send_forward, "expert", split_axis=0, concat_axis=0, tiled=True)
    blocked = got_forward.reshape(sources, local_count, capacity, width)
    pre_act = jnp.einsum("jecd,edf->jecf", blocked, up_weight, preferred_element_type=jnp.float32)
    hidden = jax.nn.silu(pre_act).astype(jnp.bfloat16)
    result = jnp.einsum(
        "jecf,efd->jecd", hidden, down_weight, preferred_element_type=jnp.float32
    ).astype(jnp.bfloat16)
    back_forward = lax.all_to_all(
        result.reshape(sources, local_count * capacity, width),
        "expert",
        split_axis=0,
        concat_axis=0,
        tiled=True,
    )
    got_backward = lax.all_to_all(send_backward, "expert", split_axis=0, concat_axis=0, tiled=True)
    blocked = got_backward.reshape(sources, local_count, capacity, width)
    hidden_grad = jnp.einsum(
        "jecd,efd->jecf", blocked, down_weight, preferred_element_type=jnp.float32
    )
    hidden_rounded = lax.optimization_barrier(jax.nn.silu(saved_pre).astype(jnp.bfloat16)).astype(
        jnp.float32
    )
    inner_sums = jnp.sum(hidden_grad * hidden_rounded, axis=-1).astype(jnp.bfloat16)
    sigmoid_pre = jax.nn.sigmoid(saved_pre)
    pre_grad = (hidden_grad * sigmoid_pre * (1.0 + saved_pre * (1.0 - sigmoid_pre))).astype(
        jnp.bfloat16
    )
    input_rows = jnp.einsum(
        "jecf,edf->jecd", pre_grad, up_weight, preferred_element_type=jnp.float32
    ).astype(jnp.bfloat16)
    backward_rows, inner_sums = (
        input_rows.reshape(sources, local_count * capacity, width),
        inner_sums.reshape(sources, local_count * capacity),
    )
    back_rows, back_sums = (
        lax.all_to_all(backward_rows, "expert", split_axis=0, concat_axis=0, tiled=True),
        lax.all_to_all(inner_sums, "expert", split_axis=0, concat_axis=0, tiled=True),
    )
    expert_sum = jnp.dot(
        mixing, back_forward.reshape(slots, width), preferred_element_type=jnp.float32
    )
    forward_output = (widened + expert_sum).astype(jnp.bfloat16)
    normed_grad = jnp.dot(
        saved_mixing, back_rows.reshape(slots, width), preferred_element_type=jnp.float32
    )
    route_sums = jnp.einsum(
        "tks,s->tk", saved_table, back_sums.reshape(slots).astype(jnp.float32), precision=HIGH
    )
    chosen_grad = saved_shares * (
        route_sums - jnp.sum(saved_shares * route_sums, axis=1, keepdims=True)
    )
    route_hits = (backward_routes[0][..., None] == jnp.arange(experts, dtype=jnp.int32)).astype(
        jnp.float32
    )
    logit_grad = jnp.einsum("tk,tke->te", chosen_grad, route_hits, precision=HIGH)
    normed_grad = normed_grad + jnp.dot(
        logit_grad, router_mat.astype(jnp.float32).T, precision=HIGH
    )
    gained_grad = normed_grad * gain_row.astype(jnp.float32)
    input_grad = saved_rms[:, None] * gained_grad - saved_wide * (saved_rms**3)[
        :, None
    ] * jnp.mean(saved_wide * gained_grad, axis=-1, keepdims=True)
    input_gradient = (upstream.astype(jnp.float32) + input_grad).astype(jnp.bfloat16)
    return (forward_output[None], input_gradient[None])


def solution(mesh):
    return jax.shard_map(
        on_device,
        mesh=mesh,
        in_specs=(
            P("section", "expert", None),
            P("expert", None),
            P("section", "expert", None),
            P("section", "expert", None),
            P("expert", None),
            P("section", "expert", None),
            P("section", "expert", None),
            P("section", None, "expert", None, None),
            P("section", None),
            P("section", None, None),
            P("expert", None, None),
            P("expert", None, None),
        ),
        out_specs=(P("section", "expert", None), P("section", "expert", None)),
        check_vma=False,
    )
```

profile of v0, /device:TPU:1, one launch (start us, length us, event | category | flops | bytes accessed | tf_op | source)
XLA Modules:
  0.0 530.2 jit_solution(10388317577833384974)
XLA Ops:
  0.6 4.1 collective-permute-start
  4.7 1.3 collective-permute-start.1
  6.0 0.7 bitcast_or_fusion
  6.7 0.8 copy.70
  7.5 0.7 mul.191
  8.2 0.7 bitcast_or_fusion.1
  8.9 1.1 fusion.48
  10.0 0.1 eq.84
  10.2 0.2 reduce_window_sum.18
  10.4 1.2 fusion.64
  11.7 0.2 select_reduce_fusion.2
  12.3 1.3 gather_fusion.1
  13.8 0.1 reduce_sum.129
  14.1 0.2 fusion.56
  14.3 0.3 fusion.69
  14.6 1.3 gather_fusion
  16.3 0.4 convolution_convert_fusion
  16.7 1.3 reshape.195
  18.0 30.0 %all-to-all-start.2 = ((bf16[64,3,2048]{2,1,0:T(4,128)(2,1)}), bf16[64,3,2048]{2,1,0:T(4,128)(2,1)S(1)}, u32[]{:S(2)}, u32[]{:S(2)}) async-start(bf16[64,3,2048]{2,1,0:T(4,128)(2,1)} %reshape.195), calls=%async_computation.2 | async-start | bytes 2097152 | tf_op jit(solution)/shard_map/all_to_all | solution.py:99
  48.3 0.2 reduce_window_sum.17
  48.5 0.2 select_reduce_fusion.3
  49.1 0.4 convolution_convert_fusion.1
  49.5 1.3 reshape.190
  50.8 105.1 %all-to-all-done.2 = bf16[64,3,2048]{2,1,0:T(4,128)(2,1)S(1)} async-done(((bf16[64,3,2048]{2,1,0:T(4,128)(2,1)}), bf16[64,3,2048]{2,1,0:T(4,128)(2,1)S(1)}, u32[]{:S(2)}, u32[]{:S(2)}) %all-to-all-start.2) | async-done | bytes 786464 | tf_op jit(solution)/shard_map/all_to_all | solution.py:99
  155.9 5.7 %all-to-all-start = ((bf16[64,3,2048]{2,1,0:T(4,128)(2,1)}), bf16[64,3,2048]{2,1,0:T(4,128)(2,1)S(1)}, u32[]{:S(2)}, u32[]{:S(2)}) async-start(bf16[64,3,2048]{2,1,0:T(4,128)(2,1)} %reshape.190), calls=%async_computation | async-start | bytes 2097152 | tf_op jit(solution)/shard_map/all_to_all | solution.py:85
  161.6 0.2 fusion.29
  161.9 4.9 multiply_reduce_fusion
  166.7 0.7 copy.76
  167.5 102.1 %all-to-all-done = bf16[64,3,2048]{2,1,0:T(4,128)(2,1)S(1)} async-done(((bf16[64,3,2048]{2,1,0:T(4,128)(2,1)}), bf16[64,3,2048]{2,1,0:T(4,128)(2,1)S(1)}, u32[]{:S(2)}, u32[]{:S(2)}) %all-to-all-start) | async-done | bytes 786464 | tf_op jit(solution)/shard_map/all_to_all | solution.py:85
  269.6 5.7 %all-to-all-start.4 = ((bf16[64,1,3]{2,1,0:T(2,128)(2,1)}), bf16[64,1,3]{2,1,0:T(2,128)(2,1)S(1)}, u32[]{:S(2)}, u32[]{:S(2)}) async-start(bf16[64,1,3]{2,1,0:T(2,128)(2,1)} %copy.76), calls=%async_computation.4 | async-start | bytes 65536 | tf_op jit(solution)/shard_map/all_to_all | solution.py:121
  275.3 4.1 fusion.8
  279.3 1.7 copy.75
  281.0 16.6 %all-to-all-done.4 = bf16[64,1,3]{2,1,0:T(2,128)(2,1)S(1)} async-done(((bf16[64,1,3]{2,1,0:T(2,128)(2,1)}), bf16[64,1,3]{2,1,0:T(2,128)(2,1)S(1)}, u32[]{:S(2)}, u32[]{:S(2)}) %all-to-all-start.4) | async-done | bytes 416 | tf_op jit(solution)/shard_map/all_to_all | solution.py:121
  297.6 5.7 %all-to-all-start.3 = ((bf16[64,3,2048]{2,1,0:T(4,128)(2,1)}), bf16[64,3,2048]{2,1,0:T(4,128)(2,1)S(1)}, u32[]{:S(2)}, u32[]{:S(2)}) async-start(bf16[64,3,2048]{2,1,0:T(4,128)(2,1)} %copy.75), calls=%async_computation.3 | async-start | bytes 2097152 | tf_op jit(solution)/shard_map/all_to_all | solution.py:120
  303.3 5.8 %fusion.11 = bf16[64,3,2048]{2,0,1:T(8,128)(2,1)S(1)} fusion(bf16[1,1024,2048]{2,1,0:T(8,128)(2,1)} %param.25, bf16[1,2048,1024]{2,1,0:T(8,128)(2,1)} %param.24, bf16[64,3,2048]{2,1,0:T(4,128)(2,1)S(1)} %all-to-all-done), kind=kOutput, calls=%fused_computation.11 | convolution fusion | flops 1611988992 | bytes 9961472 | tf_op jit(solution)/shard_map/jecf,efd->jecd/dot_general | solution.py:89
  309.1 1.7 copy.69
  310.8 100.7 %all-to-all-done.3 = bf16[64,3,2048]{2,1,0:T(4,128)(2,1)S(1)} async-done(((bf16[64,3,2048]{2,1,0:T(4,128)(2,1)}), bf16[64,3,2048]{2,1,0:T(4,128)(2,1)S(1)}, u32[]{:S(2)}, u32[]{:S(2)}) %all-to-all-start.3) | async-done | bytes 786464 | tf_op jit(solution)/shard_map/all_to_all | solution.py:120
  411.5 7.1 %all-to-all-start.1 = ((bf16[64,3,2048]{2,1,0:T(4,128)(2,1)}), bf16[64,3,2048]{2,1,0:T(4,128)(2,1)S(1)}, u32[]{:S(2)}, u32[]{:S(2)}) async-start(bf16[64,3,2048]{2,1,0:T(4,128)(2,1)} %copy.69), calls=%async_computation.1 | async-start | bytes 2097152 | tf_op jit(solution)/shard_map/all_to_all | solution.py:92
  418.8 0.1 reshape.237
  419.0 0.2 fusion.73
  419.4 0.4 fusion.74
  419.8 0.7 reshape.197
  420.5 0.3 fusion.98
  420.8 0.5 fusion.53
  421.3 105.4 %all-to-all-done.1 = bf16[64,3,2048]{2,1,0:T(4,128)(2,1)S(1)} async-done(((bf16[64,3,2048]{2,1,0:T(4,128)(2,1)}), bf16[64,3,2048]{2,1,0:T(4,128)(2,1)S(1)}, u32[]{:S(2)}, u32[]{:S(2)}) %all-to-all-start.1) | async-done | bytes 786464 | tf_op jit(solution)/shard_map/all_to_all | solution.py:92
  526.7 0.7 reshape.194
  527.4 1.0 fusion.16
  528.4 1.9 fusion.66
  (56 shorter events, 2.3 us)
Async XLA Ops:
  0.6 9.8 %copy-start = (bf16[1,2048,64]{1,2,0:T(8,128)(2,1)S(1)}, bf16[1,2048,64]{1,2,0:T(8,128)(2,1)}, u32[]{:S(2)}) copy-start(bf16[1,2048,64]{1,2,0:T(8,128)(2,1)} %param.23) | copy-start | bytes 786436
  0.6 13.4 %collective-permute-start = (bf16[64,2048]{1,0:T(8,128)(2,1)}, bf16[64,2048]{1,0:T(8,128)(2,1)S(1)}, u32[]{:S(2)}, u32[]{:S(2)}) collective-permute-start(bf16[64,2048]{1,0:T(8,128)(2,1)} %bitcast.152), channel_id=1, source_target_pairs={{0,64},{64,128},{128,192},{192,256},{256,320},{320,384},{384,448},... | collective-permute-start | bytes 786440 | tf_op jit(solution)/shard_map/ppermute | solution.py:13
  4.7 11.6 %collective-permute-start.1 = (bf16[64,2048]{1,0:T(8,128)(2,1)}, bf16[64,2048]{1,0:T(8,128)(2,1)S(1)}, u32[]{:S(2)}, u32[]{:S(2)}) collective-permute-start(bf16[64,2048]{1,0:T(8,128)(2,1)} %bitcast.153), channel_id=1, source_target_pairs={{64,0},{128,64},{192,128},{256,192},{320,256},{384,320},{448,384},... | collective-permute-start | bytes 786440 | tf_op jit(solution)/shard_map/ppermute | solution.py:13
  12.3 1.7 copy-start.9
  12.3 1.8 copy-start.8
  14.3 34.8 %copy-start.2 = (bf16[64,2048]{1,0:T(8,128)(2,1)}, bf16[64,2048]{1,0:T(8,128)(2,1)S(1)}, u32[]{:S(2)}) copy-start(bf16[64,2048]{1,0:T(8,128)(2,1)S(1)} %get-tuple-element.14) | copy-start | bytes 786436
  14.6 1.5 copy-start.10
  14.6 1.7 copy-start.4
  16.3 1.7 copy-start.6
  18.0 143.6 %copy-start.7 = (bf16[1,64,1,3,1024]{4,1,3,2,0:T(8,128)(2,1)S(1)}, bf16[1,64,1,3,1024]{4,1,3,2,0:T(8,128)(2,1)}, u32[]{:S(2)}) copy-start(bf16[1,64,1,3,1024]{4,1,3,2,0:T(8,128)(2,1)} %param.21) | copy-start | bytes 1179652
  18.0 137.9 %all-to-all-start.2 = ((bf16[64,3,2048]{2,1,0:T(4,128)(2,1)}), bf16[64,3,2048]{2,1,0:T(4,128)(2,1)S(1)}, u32[]{:S(2)}, u32[]{:S(2)}) async-start(bf16[64,3,2048]{2,1,0:T(4,128)(2,1)} %reshape.195), calls=%async_computation.2 | async-start | bytes 2097152 | tf_op jit(solution)/shard_map/all_to_all | solution.py:99
  155.9 113.6 %all-to-all-start = ((bf16[64,3,2048]{2,1,0:T(4,128)(2,1)}), bf16[64,3,2048]{2,1,0:T(4,128)(2,1)S(1)}, u32[]{:S(2)}, u32[]{:S(2)}) async-start(bf16[64,3,2048]{2,1,0:T(4,128)(2,1)} %reshape.190), calls=%async_computation | async-start | bytes 2097152 | tf_op jit(solution)/shard_map/all_to_all | solution.py:85
  269.6 28.0 %all-to-all-start.4 = ((bf16[64,1,3]{2,1,0:T(2,128)(2,1)}), bf16[64,1,3]{2,1,0:T(2,128)(2,1)S(1)}, u32[]{:S(2)}, u32[]{:S(2)}) async-start(bf16[64,1,3]{2,1,0:T(2,128)(2,1)} %copy.76), calls=%async_computation.4 | async-start | bytes 65536 | tf_op jit(solution)/shard_map/all_to_all | solution.py:121
  297.6 113.9 %all-to-all-start.3 = ((bf16[64,3,2048]{2,1,0:T(4,128)(2,1)}), bf16[64,3,2048]{2,1,0:T(4,128)(2,1)S(1)}, u32[]{:S(2)}, u32[]{:S(2)}) async-start(bf16[64,3,2048]{2,1,0:T(4,128)(2,1)} %copy.75), calls=%async_computation.3 | async-start | bytes 2097152 | tf_op jit(solution)/shard_map/all_to_all | solution.py:120
  309.1 111.7 %copy-start.1 = (bf16[1,64,2048]{2,1,0:T(8,128)(2,1)S(1)}, bf16[1,64,2048]{2,1,0:T(8,128)(2,1)}, u32[]{:S(2)}) copy-start(bf16[1,64,2048]{2,1,0:T(8,128)(2,1)} %param.19) | copy-start | bytes 786436
  411.5 115.2 %all-to-all-start.1 = ((bf16[64,3,2048]{2,1,0:T(4,128)(2,1)}), bf16[64,3,2048]{2,1,0:T(4,128)(2,1)S(1)}, u32[]{:S(2)}, u32[]{:S(2)}) async-start(bf16[64,3,2048]{2,1,0:T(4,128)(2,1)} %copy.69), calls=%async_computation.1 | async-start | bytes 2097152 | tf_op jit(solution)/shard_map/all_to_all | solution.py:92
  420.5 106.9 %copy-start.3 = (bf16[64,2048]{1,0:T(8,128)(2,1)S(1)}, bf16[64,2048]{1,0:T(8,128)(2,1)}, u32[]{:S(2)}) copy-start(bf16[64,2048]{1,0:T(8,128)(2,1)} %copy-done.2) | copy-start | bytes 786436
  420.8 107.6 %copy-start.5 = (bf16[64,2048]{1,0:T(8,128)(2,1)S(1)}, bf16[64,2048]{1,0:T(8,128)(2,1)}, u32[]{:S(2)}) copy-start(bf16[64,2048]{1,0:T(8,128)(2,1)} %param.18) | copy-start | bytes 786436
where the time goes:
time: 536 us; the launch traced here: 530 us
  waiting for transfers between devices  430 us (80%)
  starting transfers between devices  59.6 us (11%)
  matrix products  19.3 us (4%)
  local copies, waits for them, and re-layouts  13.5 us (3%)
  other arithmetic  6.81 us (1%)
    all_to_all x1, waiting for transfers between devices, on_device(): lax.all_to_all(result.reshape(sources, local_count * capacity, width), 'e...  105 us
    all_to_all x1, waiting for transfers between devices, on_device(): lax.all_to_all(send_backward, 'expert', split_axis=0, concat_axis=0, tile...  105 us
    all_to_all x1, waiting for transfers between devices, on_device(): lax.all_to_all(send_forward, 'expert', split_axis=0, concat_axis=0, tiled...  102 us
    all_to_all x1, waiting for transfers between devices, on_device(): lax.all_to_all(backward_rows, 'expert', split_axis=0, concat_axis=0, tile...  101 us
    all_to_all x1, starting transfers between devices, on_device(): lax.all_to_all(send_backward, 'expert', split_axis=0, concat_axis=0, tile...  30 us
    all_to_all x1, waiting for transfers between devices, on_device(): lax.all_to_all(inner_sums, 'expert', split_axis=0, concat_axis=0, tiled=T...  16.6 us
  transfers between devices with their start and end apart: 7, of which 5 were waited for; matrix products, arithmetic and copies ran while one was open for 6% of the time, Pallas kernels for 0%

commit v1 on v0

--- a/solution.py
+++ b/solution.py
@@ -1,10 +1,15 @@
+import functools
+
 import jax
 import jax.numpy as jnp
 from jax import lax
+from jax.experimental import pallas as pl
+from jax.experimental.pallas import tpu as pltpu
 from jax.sharding import PartitionSpec as P
 
 EPS = 1e-06
 HIGH = lax.Precision.HIGHEST
+LANE = 128
 
 
 def from_behind(block, axis, distance):
@@ -37,6 +42,261 @@
     placing = jnp.sum(slot_table, axis=1).astype(jnp.bfloat16)
     mixing = jnp.sum(slot_table * rounded[..., None], axis=1).astype(jnp.bfloat16)
     return (widened, inv_rms, normed, shares, slot_table, placing, mixing)
+
+
+def relay_kernel(
+    devices,
+    capacity,
+    send_f,
+    send_b,
+    pre_hbm,
+    up_hbm,
+    down_hbm,
+    out_f,
+    out_b,
+    out_s,
+    pre,
+    up,
+    down,
+    got_f,
+    got_b,
+    ret_f,
+    ret_b,
+    ret_s,
+    wide,
+    mid,
+    load_sem,
+    send_sem,
+    recv_sem,
+    small_send,
+    small_recv,
+):
+    me = lax.axis_index("expert")
+    chips = devices // 2
+    spot, core = me // 2, lax.rem(me, 2)
+    hidden_size, width = down.shape
+    rows = devices * capacity
+    sub = width // LANE
+    entry = capacity * sub
+    group = 32
+    tile = 256
+
+    loads = [
+        pltpu.make_async_copy(pre_hbm, pre, load_sem.at[0]),
+        pltpu.make_async_copy(down_hbm, down, load_sem.at[1]),
+        pltpu.make_async_copy(up_hbm, up, load_sem.at[2]),
+    ]
+    for load in loads:
+        load.start()
+
+    barrier = pltpu.get_barrier_semaphore()
+    for step in range(1, devices):
+        pl.semaphore_signal(
+            barrier, 1, device_id={"expert": lax.rem(me + step, devices)}
+        )
+    pl.semaphore_wait(barrier, devices - 1)
+
+    peers = []
+    for distance in range(chips // 2, -1, -1):
+        ways = (1,) if distance in (0, chips // 2) else (1, -1)
+        for way in ways:
+            for other in (0, 1):
+                if distance or other:
+                    place = lax.rem(spot + way * distance + chips, chips)
+                    peers.append(place * 2 + lax.rem(core + other, 2))
+
+    def part(ref, device):
+        return ref.at[pl.ds(pl.multiple_of(device * entry, entry), entry), :]
+
+    def exchange(stage, source, target):
+        copies = []
+        for number, peer in enumerate(peers):
+            copy = pltpu.make_async_remote_copy(
+                src_ref=part(source, peer),
+                dst_ref=part(target, me),
+                send_sem=send_sem.at[stage, number],
+                recv_sem=recv_sem.at[stage, number],
+                device_id={"expert": peer},
+            )
+            copy.start()
+            copies.append(copy)
+        own = pl.ds(pl.multiple_of(me * entry, entry), entry)
+        target[own, :] = source[own, :]
+        return copies
+
+    def arrive(copies):
+        for copy in copies:
+            copy.wait_recv()
+
+    def iota(shape, axis):
+        return lax.broadcasted_iota(jnp.int32, shape, axis)
+
+    def onehot(condition):
+        return jnp.where(condition, 1.0, 0.0).astype(jnp.bfloat16)
+
+    side = group * sub
+    to_wide = onehot(
+        iota((side, side), 1)
+        == lax.rem(iota((side, side), 0), group) * sub + iota((side, side), 0) // group
+    )
+    to_lanes = onehot(
+        iota((side, side), 0)
+        == lax.rem(iota((side, side), 1), group) * sub + iota((side, side), 1) // group
+    )
+
+    def widen(source):
+        @pl.loop(0, rows // group)
+        def _(number):
+            block = source[pl.ds(pl.multiple_of(number * side, side), side), :]
+            moved = jnp.dot(to_wide, block, preferred_element_type=jnp.float32).astype(
+                jnp.bfloat16
+            )
+            here = pl.ds(pl.multiple_of(number * group, group), group)
+            for k in range(sub):
+                wide[here, k * LANE : (k + 1) * LANE] = moved[
+                    k * group : (k + 1) * group, :
+                ]
+
+    def narrow(target):
+        @pl.loop(0, rows // group)
+        def _(number):
+            here = pl.ds(pl.multiple_of(number * group, group), group)
+            block = jnp.concatenate(
+                [wide[here, k * LANE : (k + 1) * LANE] for k in range(sub)], axis=0
+            )
+            target[pl.ds(pl.multiple_of(number * side, side), side), :] = jnp.dot(
+                to_lanes, block, preferred_element_type=jnp.float32
+            ).astype(jnp.bfloat16)
+
+    def columns(number):
+        return pl.ds(pl.multiple_of(number * tile, tile), tile)
+
+    def transposed(left, right):
+        return lax.dot_general(
+            left, right, (((1,), (1,)), ((), ())), preferred_element_type=jnp.float32
+        )
+
+    sent_b = exchange(0, send_b, got_b)
+    sent_f = exchange(1, send_f, got_f)
+
+    for load in loads:
+        load.wait()
+    arrive(sent_b)
+    widen(got_b)
+    pick = onehot(
+        iota((rows, rows), 1)
+        == lax.rem(iota((rows, rows), 0), capacity) * devices
+        + iota((rows, rows), 0) // capacity
+    )
+
+    def back_tile(number, inner):
+        grad = transposed(wide[...], down[columns(number), :])
+        value = jnp.dot(
+            pick, pre[:, columns(number)], preferred_element_type=jnp.float32
+        )
+        gate = jax.nn.sigmoid(value)
+        rounded = (value * gate).astype(jnp.bfloat16).astype(jnp.float32)
+        mid[:, columns(number)] = (
+            grad * gate * (1.0 + value * (1.0 - gate))
+        ).astype(jnp.bfloat16)
+        return inner + jnp.sum(grad * rounded, axis=1, keepdims=True)
+
+    inner = lax.fori_loop(
+        0, hidden_size // tile, back_tile, jnp.zeros((rows, 1), jnp.float32)
+    )
+    spread = jnp.where(
+        iota((rows, LANE), 1) == lax.rem(iota((rows, LANE), 0), capacity), inner, 0.0
+    ).astype(jnp.bfloat16)
+    gather = onehot(
+        iota((devices, rows), 0) == iota((devices, rows), 1) // capacity
+    )
+    sums = jnp.dot(gather, spread, preferred_element_type=jnp.float32)
+    for number in range(devices):
+        ret_s[number] = sums[number : number + 1, :]
+
+    @pl.loop(0, width // tile)
+    def _(number):
+        wide[:, columns(number)] = transposed(
+            mid[...], up[columns(number), :]
+        ).astype(jnp.bfloat16)
+
+    narrow(ret_b)
+    small = []
+    for number, peer in enumerate(peers):
+        copy = pltpu.make_async_remote_copy(
+            src_ref=ret_s.at[peer],
+            dst_ref=out_s.at[me],
+            send_sem=small_send.at[number],
+            recv_sem=small_recv.at[number],
+            device_id={"expert": peer},
+        )
+        copy.start()
+        small.append(copy)
+    out_s[me] = ret_s[me]
+    back_b = exchange(2, ret_b, out_b)
+
+    arrive(sent_f)
+    widen(got_f)
+
+    @pl.loop(0, hidden_size // tile)
+    def _(number):
+        value = jnp.dot(
+            wide[...], up[:, columns(number)], preferred_element_type=jnp.float32
+        )
+        mid[:, columns(number)] = jax.nn.silu(value).astype(jnp.bfloat16)
+
+    @pl.loop(0, width // tile)
+    def _(number):
+        wide[:, columns(number)] = jnp.dot(
+            mid[...], down[:, columns(number)], preferred_element_type=jnp.float32
+        ).astype(jnp.bfloat16)
+
+    narrow(ret_f)
+    back_f = exchange(3, ret_f, out_f)
+    arrive(small)
+    arrive(back_b)
+    arrive(back_f)
+    for copy in sent_b + sent_f + small + back_b + back_f:
+        copy.wait_send()
+
+
+def relay(send_f, send_b, pre, up_mat, down_mat, devices, capacity):
+    lanes = send_f.shape
+    hidden_size, width = down_mat.shape
+    rows = devices * capacity
+    vmem = pl.BlockSpec(memory_space=pltpu.VMEM)
+    anywhere = pl.BlockSpec(memory_space=pl.ANY)
+    row_type = jax.ShapeDtypeStruct(lanes, jnp.bfloat16)
+    return pl.pallas_call(
+        functools.partial(relay_kernel, devices, capacity),
+        out_shape=(
+            row_type,
+            row_type,
+            jax.ShapeDtypeStruct((devices, 1, LANE), jnp.float32),
+        ),
+        in_specs=[vmem, vmem, anywhere, anywhere, anywhere],
+        out_specs=(vmem, vmem, vmem),
+        scratch_shapes=[
+            pltpu.VMEM(pre.shape, jnp.bfloat16),
+            pltpu.VMEM(up_mat.shape, jnp.bfloat16),
+            pltpu.VMEM(down_mat.shape, jnp.bfloat16),
+            pltpu.VMEM(lanes, jnp.bfloat16),
+            pltpu.VMEM(lanes, jnp.bfloat16),
+            pltpu.VMEM(lanes, jnp.bfloat16),
+            pltpu.VMEM(lanes, jnp.bfloat16),
+            pltpu.VMEM((devices, 1, LANE), jnp.float32),
+            pltpu.VMEM((rows, width), jnp.bfloat16),
+            pltpu.VMEM((rows, hidden_size), jnp.bfloat16),
+            pltpu.SemaphoreType.DMA((3,)),
+            pltpu.SemaphoreType.DMA((4, devices)),
+            pltpu.SemaphoreType.DMA((4, devices)),
+            pltpu.SemaphoreType.DMA((devices,)),
+            pltpu.SemaphoreType.DMA((devices,)),
+        ],
+        compiler_params=pltpu.CompilerParams(
+            collective_id=0, has_side_effects=True, vmem_limit_bytes=48 << 20
+        ),
+    )(send_f, send_b, pre, up_mat, down_mat)
 
 
 def on_device(
@@ -58,7 +318,6 @@
     sources = lax.axis_size("expert")
     experts = router.shape[2]
     capacity = pre_activation.shape[3]
-    local_count = up_weight.shape[0]
     width = up_weight.shape[1]
     slots = experts * capacity
     gain_row = norm_gain[0]
@@ -76,50 +335,20 @@
     send_forward = jnp.einsum(
         "ts,td->sd", placing, normed, preferred_element_type=jnp.float32
     ).astype(jnp.bfloat16)
-    send_forward = send_forward.reshape(sources, local_count * capacity, width)
     send_backward = jnp.einsum(
         "ts,td->sd", saved_placing, upstream, preferred_element_type=jnp.float32
     ).astype(jnp.bfloat16)
-    send_backward = send_backward.reshape(sources, local_count * capacity, width)
-    saved_pre = pre_activation[0].astype(jnp.float32)
-    got_forward = lax.all_to_all(send_forward, "expert", split_axis=0, concat_axis=0, tiled=True)
-    blocked = got_forward.reshape(sources, local_count, capacity, width)
-    pre_act = jnp.einsum("jecd,edf->jecf", blocked, up_weight, preferred_element_type=jnp.float32)
-    hidden = jax.nn.silu(pre_act).astype(jnp.bfloat16)
-    result = jnp.einsum(
-        "jecf,efd->jecd", hidden, down_weight, preferred_element_type=jnp.float32
-    ).astype(jnp.bfloat16)
-    back_forward = lax.all_to_all(
-        result.reshape(sources, local_count * capacity, width),
-        "expert",
-        split_axis=0,
-        concat_axis=0,
-        tiled=True,
-    )
-    got_backward = lax.all_to_all(send_backward, "expert", split_axis=0, concat_axis=0, tiled=True)
-    blocked = got_backward.reshape(sources, local_count, capacity, width)
-    hidden_grad = jnp.einsum(
-        "jecd,efd->jecf", blocked, down_weight, preferred_element_type=jnp.float32
-    )
-    hidden_rounded = lax.optimization_barrier(jax.nn.silu(saved_pre).astype(jnp.bfloat16)).astype(
-        jnp.float32
-    )
-    inner_sums = jnp.sum(hidden_grad * hidden_rounded, axis=-1).astype(jnp.bfloat16)
-    sigmoid_pre = jax.nn.sigmoid(saved_pre)
-    pre_grad = (hidden_grad * sigmoid_pre * (1.0 + saved_pre * (1.0 - sigmoid_pre))).astype(
-        jnp.bfloat16
-    )
-    input_rows = jnp.einsum(
-        "jecf,edf->jecd", pre_grad, up_weight, preferred_element_type=jnp.float32
-    ).astype(jnp.bfloat16)
-    backward_rows, inner_sums = (
-        input_rows.reshape(sources, local_count * capacity, width),
-        inner_sums.reshape(sources, local_count * capacity),
-    )
-    back_rows, back_sums = (
-        lax.all_to_all(backward_rows, "expert", split_axis=0, concat_axis=0, tiled=True),
-        lax.all_to_all(inner_sums, "expert", split_axis=0, concat_axis=0, tiled=True),
-    )
+    saved_pre = pre_activation[0, :, 0].transpose(1, 0, 2).reshape(slots, -1)
+    back_forward, back_rows, back_sums = relay(
+        send_forward.reshape(-1, LANE),
+        send_backward.reshape(-1, LANE),
+        saved_pre,
+        up_weight[0],
+        down_weight[0],
+        sources,
+        capacity,
+    )
+    back_sums = back_sums[:, 0, :capacity]
     expert_sum = jnp.dot(
         mixing, back_forward.reshape(slots, width), preferred_element_type=jnp.float32
     )

time: 536 us -> 339 us (0.63)
  waiting for transfers between devices: 430 us -> 0.01 us
  Pallas kernels: 0 us -> 310 us
  starting transfers between devices: 59.6 us -> 5.37 us
  matrix products: 19.3 us -> 5.63 us
    all_to_all x5 -> x0, waiting for transfers between devices: 430 us -> none  [the longest x1 105 us: on_device(): lax.all_to_all(result.reshape(sources, local_count * capacity, width), 'e...]
    pallas_call x0 -> x1, Pallas kernels: none -> 310 us  [relay(): pl.pallas_call(functools.partial(relay_kernel, devices, capacity), out_sh...]
    all_to_all x5 -> x0, starting transfers between devices: 54.2 us -> none  [the longest x1 30 us: on_device(): lax.all_to_all(send_backward, 'expert', split_axis=0, concat_axis=0, tile...]
    dot_general x3 -> x0, matrix products: 14.7 us -> none  [the longest x1 5.76 us: on_device(): jnp.einsum('jecf,efd->jecd', hidden, down_weight, preferred_element_type=...]
  transfers between devices with their start and end apart: 7 -> 2, of which waited for: 5 -> 0; matrix products, arithmetic and copies ran while one was open for 6% -> 4% of each run, Pallas kernels for 0% -> 0%
where the time goes in v1:
time: 339 us; the launch traced here: 336 us
  Pallas kernels  310 us (91%)
  local copies, waits for them, and re-layouts  8.51 us (3%)
  other arithmetic  6.28 us (2%)
  matrix products  5.63 us (2%)
  starting transfers between devices  5.37 us (2%)
    pallas_call x1, Pallas kernels, relay(): pl.pallas_call(functools.partial(relay_kernel, devices, capacity), out_sh...  310 us
  transfers between devices with their start and end apart: 2, of which 0 were waited for; matrix products, arithmetic and copies ran while one was open for 4% of the time, Pallas kernels for 0%

profile of v1, /device:TPU:1, one launch (start us, length us, event | category | flops | bytes accessed | tf_op | source)
XLA Modules:
  0.0 336.5 jit_solution(8777100872347840118)
XLA Ops:
  0.6 4.1 %collective-permute-start = (bf16[64,2048]{1,0:T(8,128)(2,1)}, bf16[64,2048]{1,0:T(8,128)(2,1)S(1)}, u32[]{:S(2)}, u32[]{:S(2)}) collective-permute-start(bf16[64,2048]{1,0:T(8,128)(2,1)} %bitcast.98), channel_id=1, source_target_pairs={{0,64},{64,128},{128,192},{192,256},{256,320},{320,384},{384,448},... | collective-permute-start | bytes 786440 | tf_op jit(solution)/shard_map/ppermute | solution.py:18
  4.7 1.3 collective-permute-start.1
  6.0 0.7 bitcast_or_fusion.1
  6.7 0.8 copy.40
  7.5 0.7 bitcast_or_fusion
  8.2 0.8 copy.44
  8.9 0.7 mul.150
  9.7 1.1 fusion.6
  10.8 0.1 eq.76
  11.0 0.2 reduce_window_sum.17
  11.2 0.2 select_reduce_fusion.3
  11.4 0.1 reduce_sum.113
  11.6 0.7 fusion.44
  12.3 0.1 eq.83
  12.5 0.2 reduce_window_sum.18
  12.7 1.2 fusion.18
  13.9 0.2 select_reduce_fusion.2
  14.1 0.1 copy.42
  14.2 0.1 reshape.120
  14.3 0.1 copy.46
  14.4 0.1 reshape.125
  14.6 1.3 gather_fusion.1
  15.9 0.1 reshape.128
  16.1 0.1 reduce_sum.119
  16.3 0.1 copy.48
  16.5 0.2 fusion.14
  16.7 0.3 fusion.23
  17.0 1.3 gather_fusion
  18.3 0.1 reshape.123
  18.5 0.1 select_reduce_fusion.1
  18.7 0.4 convolution_convert_fusion.1
  19.1 0.4 reshape.89.send_f
  19.5 0.1 select_reduce_fusion
  19.6 0.4 convolution_convert_fusion
  20.0 0.4 reshape.90.send_b
  20.4 1.0 copy-done.1
  21.4 309.6 %shard_map.131 = (bf16[3072,128]{1,0:T(8,128)(2,1)S(1)}, bf16[3072,128]{1,0:T(8,128)(2,1)S(1)}, f32[64,1,128]{2,1,0:T(1,128)S(1)}) custom-call(bf16[3072,128]{1,0:T(8,128)(2,1)S(1)} %reshape.89.send_f, bf16[3072,128]{1,0:T(8,128)(2,1)S(1)} %reshape.90.send_b, bf16[192,1024]{1,0:T(8,128)(2,1)S(1)} %bitcast.87, bf16[2048,1024]{1,0:T(8,128)(2,1)} %bitcast.88, ...), custom_call_target="tpu_custom_call" | custom-call | tf_op jit(solution)/shard_map/pallas_call | solution.py:270
  331.1 0.1 reshape.129
  331.3 0.2 fusion.27
  331.5 0.1 multiply_reduce_fusion
  331.6 0.1 copy.50
  331.7 0.3 reshape.93
  332.0 0.4 fusion.28
  332.5 0.3 fusion.50
  332.7 1.5 fusion.11
  334.2 0.3 reshape.92
  334.6 1.0 fusion.2
  335.5 0.9 fusion.20
  (42 shorter events, 0.7 us)
Async XLA Ops:
  0.6 12.1 %copy-start = (bf16[1,2048,64]{1,2,0:T(8,128)(2,1)S(1)}, bf16[1,2048,64]{1,2,0:T(8,128)(2,1)}, u32[]{:S(2)}) copy-start(bf16[1,2048,64]{1,2,0:T(8,128)(2,1)} %param.23) | copy-start | bytes 786436
  0.6 15.8 %collective-permute-start = (bf16[64,2048]{1,0:T(8,128)(2,1)}, bf16[64,2048]{1,0:T(8,128)(2,1)S(1)}, u32[]{:S(2)}, u32[]{:S(2)}) collective-permute-start(bf16[64,2048]{1,0:T(8,128)(2,1)} %bitcast.98), channel_id=1, source_target_pairs={{0,64},{64,128},{128,192},{192,256},{256,320},{320,384},{384,448},... | collective-permute-start | bytes 786440 | tf_op jit(solution)/shard_map/ppermute | solution.py:18
  4.7 14.9 %collective-permute-start.1 = (bf16[64,2048]{1,0:T(8,128)(2,1)}, bf16[64,2048]{1,0:T(8,128)(2,1)S(1)}, u32[]{:S(2)}, u32[]{:S(2)}) collective-permute-start(bf16[64,2048]{1,0:T(8,128)(2,1)} %bitcast.99), channel_id=1, source_target_pairs={{64,0},{128,64},{192,128},{256,192},{320,256},{384,320},{448,384},... | collective-permute-start | bytes 786440 | tf_op jit(solution)/shard_map/ppermute | solution.py:18
  14.6 1.7 copy-start.10
  14.6 1.9 copy-start.9
  16.7 2.0 copy-start.3
  17.0 1.5 copy-start.11
  17.0 2.6 copy-start.5
  19.6 0.8 copy-start.7
  20.4 1.0 copy-start.1
  331.0 3.6 %copy-start.4 = (bf16[64,2048]{1,0:T(8,128)(2,1)S(1)}, bf16[64,2048]{1,0:T(8,128)(2,1)}, u32[]{:S(2)}) copy-start(bf16[64,2048]{1,0:T(8,128)(2,1)} %copy-done.3) | copy-start | bytes 786436
  331.0 4.5 %copy-start.2 = (bf16[1,64,2048]{2,1,0:T(8,128)(2,1)S(1)}, bf16[1,64,2048]{2,1,0:T(8,128)(2,1)}, u32[]{:S(2)}) copy-start(bf16[1,64,2048]{2,1,0:T(8,128)(2,1)} %param.19) | copy-start | bytes 786436
  331.0 4.5 %copy-start.6 = (bf16[64,2048]{1,0:T(8,128)(2,1)S(1)}, bf16[64,2048]{1,0:T(8,128)(2,1)}, u32[]{:S(2)}) copy-start(bf16[64,2048]{1,0:T(8,128)(2,1)} %param.18) | copy-start | bytes 786436
  332.0 3.5 %copy-start.8 = (bf16[64,2048]{1,0:T(8,128)(2,1)S(1)}, bf16[64,2048]{1,0:T(8,128)(2,1)}, u32[]{:S(2)}) copy-start(bf16[64,2048]{1,0:T(8,128)(2,1)} %copy-done.7) | copy-start | bytes 786436

commit v2 on v0

v2 whole, which is shorter than its diff:
```python
import functools

import jax
import jax.numpy as jnp
from jax import lax
from jax.experimental import pallas as pl
from jax.experimental.pallas import tpu as pltpu
from jax.sharding import PartitionSpec as P

EPS = 1e-06
HIGH = lax.Precision.HIGHEST
LANE = 128
TILE = 256
GROUP = 32


def iota(shape, axis):
    return lax.broadcasted_iota(jnp.int32, shape, axis)


def onehot(condition):
    return jnp.where(condition, 1.0, 0.0).astype(jnp.bfloat16)


def dot(left, right, precision=None):
    return jnp.dot(
        left, right, preferred_element_type=jnp.float32, precision=precision
    )


def dot_transposed(left, right, precision=None):
    return lax.dot_general(
        left,
        right,
        (((1,), (1,)), ((), ())),
        preferred_element_type=jnp.float32,
        precision=precision,
    )


def columns(number):
    return pl.ds(pl.multiple_of(number * TILE, TILE), TILE)


def relay_kernel(
    sizes,
    forward_hbm,
    backward_hbm,
    routes_b_hbm,
    loss_hbm,
    routes_f_hbm,
    embedded_hbm,
    gain_hbm,
    router_hbm,
    down_hbm,
    pre_hbm,
    up_hbm,
    saved_hbm,
    out_f,
    out_b,
    routes_b,
    loss,
    routes_f,
    embedded,
    gain,
    router,
    down,
    pre,
    up,
    saved,
    arrived,
    returned,
    tokens,
    upstream,
    normed,
    mixing,
    gained,
    send_f,
    send_b,
    got_f,
    got_b,
    ret_f,
    ret_b,
    back_f,
    back_b,
    ret_s,
    back_s,
    wide,
    mid,
    load_sem,
    send_sem,
    recv_sem,
    pass_send,
    pass_recv,
):
    devices, sections, experts, capacity = sizes
    section = lax.axis_index("section")
    me = lax.axis_index("expert")
    chips = devices // 2
    spot, core = me // 2, lax.rem(me, 2)
    hidden_size, width = down.shape
    count = tokens.shape[0]
    rows = experts * capacity
    sub = width // LANE
    entry = capacity * sub

    barrier = pltpu.get_barrier_semaphore()
    ahead = {"section": lax.rem(section + 1, sections)}
    behind = {"section": lax.rem(section + sections - 1, sections)}
    pl.semaphore_signal(barrier, 1, device_id=ahead)
    pl.semaphore_signal(barrier, 1, device_id=behind)

    @pl.loop(1, devices)
    def _(step):
        pl.semaphore_signal(
            barrier, 1, device_id={"expert": lax.rem(me + step, devices)}
        )

    pairs = (
        (routes_b_hbm, routes_b),
        (loss_hbm, loss),
        (routes_f_hbm, routes_f),
        (embedded_hbm, embedded),
        (gain_hbm, gain),
        (router_hbm, router),
        (down_hbm, down),
        (pre_hbm, pre),
        (up_hbm, up),
        (saved_hbm, saved),
    )
    loads = [
        pltpu.make_async_copy(source, target, load_sem.at[number])
        for number, (source, target) in enumerate(pairs)
    ]
    for load in loads:
        load.start()

    def peer_of(number):
        place = number + 2
        distance = chips // 2 - place // 4
        way = 2 * lax.rem(place // 2, 2) - 1
        spot_there = lax.rem(spot + way * distance + chips, chips)
        return spot_there * 2 + lax.rem(core + number, 2)

    def part(ref, device):
        return ref.at[pl.ds(pl.multiple_of(device * entry, entry), entry), :]

    def copy_of(stage, number, peer, source, target):
        if stage < 4:
            here, there = part(source, peer), part(target, me)
        else:
            here, there = source.at[peer], target.at[me]
        return pltpu.make_async_remote_copy(
            src_ref=here,
            dst_ref=there,
            send_sem=send_sem.at[stage, number],
            recv_sem=recv_sem.at[stage, number],
            device_id={"expert": peer},
        )

    partner = spot * 2 + 1 - core

    def for_peers(act):
        @pl.loop(0, devices - 2)
        def _(number):
            act(number, peer_of(number))

        act(devices - 2, partner)

    def exchange(stage, source, target):
        for_peers(
            lambda number, peer: copy_of(stage, number, peer, source, target).start()
        )
        if stage < 4:
            own = pl.ds(pl.multiple_of(me * entry, entry), entry)
            target[own, :] = source[own, :]
        else:
            target[me] = source[me]

    def arrive(stage, source, target):
        for_peers(
            lambda number, peer: copy_of(
                stage, number, peer, source, target
            ).wait_recv()
        )

    def leave(stage, source, target):
        for_peers(
            lambda number, peer: copy_of(
                stage, number, peer, source, target
            ).wait_send()
        )

    side = GROUP * sub
    to_wide = onehot(
        iota((side, side), 1)
        == lax.rem(iota((side, side), 0), GROUP) * sub + iota((side, side), 0) // GROUP
    )
    to_lanes = onehot(
        iota((side, side), 0)
        == lax.rem(iota((side, side), 1), GROUP) * sub + iota((side, side), 1) // GROUP
    )

    def widen(source):
        @pl.loop(0, rows // GROUP)
        def _(number):
            block = source[pl.ds(pl.multiple_of(number * side, side), side), :]
            moved = dot(to_wide, block).astype(jnp.bfloat16)
            here = pl.ds(pl.multiple_of(number * GROUP, GROUP), GROUP)
            for k in range(sub):
                wide[here, k * LANE : (k + 1) * LANE] = moved[
                    k * GROUP : (k + 1) * GROUP, :
                ]

    def narrow(target):
        @pl.loop(0, rows // GROUP)
        def _(number):
            here = pl.ds(pl.multiple_of(number * GROUP, GROUP), GROUP)
            block = jnp.concatenate(
                [wide[here, k * LANE : (k + 1) * LANE] for k in range(sub)], axis=0
            )
            target[pl.ds(pl.multiple_of(number * side, side), side), :] = dot(
                to_lanes, block
            ).astype(jnp.bfloat16)

    earlier = onehot(iota((count, count), 0) < iota((count, count), 1))
    identity = onehot(iota((count, count), 0) == iota((count, count), 1))

    def follow(routes):
        named = [routes[k : k + 1, :] for k in range(routes.shape[0])]
        hits = [iota((experts, count), 0) == name for name in named]
        chosen = onehot(hits[0])
        for hit in hits[1:]:
            chosen = chosen + onehot(hit)
        before = dot(chosen, earlier)
        ranks = [
            jnp.sum(jnp.where(hit, before, 0.0), axis=0, keepdims=True) for hit in hits
        ]
        slot_number = iota((rows, count), 0).astype(jnp.float32)
        places = [
            slot_number == name.astype(jnp.float32) * capacity + rank
            for name, rank in zip(named, ranks)
        ]
        return hits, ranks, places

    def dispatch(places, source, target):
        placing = onehot(places[0])
        for place in places[1:]:
            placing = placing + onehot(place)

        @pl.loop(0, width // TILE)
        def _(number):
            wide[:, columns(number)] = dot(
                placing, source[:, columns(number)]
            ).astype(jnp.bfloat16)

        narrow(target)

    def normalise(source):
        def add(number, total):
            value = source[:, columns(number)].astype(jnp.float32)
            return total + jnp.sum(value * value, axis=1, keepdims=True)

        total = lax.fori_loop(
            0, width // TILE, add, jnp.zeros((count, 1), jnp.float32)
        )
        inv_rms = lax.rsqrt(total / width + EPS)

        @pl.loop(0, width // TILE)
        def _(number):
            value = source[:, columns(number)].astype(jnp.float32)
            scale = gain[:, columns(number)].astype(jnp.float32)
            normed[:, columns(number)] = (value * inv_rms * scale).astype(jnp.bfloat16)

        return inv_rms

    def share(hits, places):
        logits = dot_transposed(router[...], normed[...])
        powers = [
            jnp.exp(jnp.sum(jnp.where(hit, logits, 0.0), axis=0, keepdims=True))
            for hit in hits
        ]
        whole = powers[0]
        for power in powers[1:]:
            whole = whole + power
        shares = [power / whole for power in powers]
        mixed = jnp.zeros((rows, count), jnp.float32)
        for portion, place in zip(shares, places):
            rounded = portion.astype(jnp.bfloat16).astype(jnp.float32)
            mixed = mixed + jnp.where(place, rounded, 0.0)
        mixed = dot_transposed(identity, mixed.astype(jnp.bfloat16))
        return shares, mixed.astype(jnp.bfloat16)

    for load in loads[:2]:
        load.wait()
    hits_b, ranks_b, places_b = follow(routes_b)
    pl.semaphore_wait(barrier, devices + 1)
    pass_back = pltpu.make_async_remote_copy(
        src_ref=backward_hbm,
        dst_ref=returned,
        send_sem=pass_send.at[0],
        recv_sem=pass_recv.at[0],
        device_id=behind,
    )
    pass_on = pltpu.make_async_remote_copy(
        src_ref=forward_hbm,
        dst_ref=arrived,
        send_sem=pass_send.at[1],
        recv_sem=pass_recv.at[1],
        device_id=ahead,
    )
    pass_back.start()
    pass_on.start()
    pass_back.wait_recv()
    upstream[...] = jnp.where(section == sections - 1, loss[...], returned[...])
    dispatch(places_b, upstream, send_b)
    exchange(0, send_b, got_b)

    for load in loads[2:6]:
        load.wait()
    hits_f, _, places_f = follow(routes_f)
    pass_on.wait_recv()
    tokens[...] = jnp.where(section == 0, embedded[...], arrived[...])
    normalise(tokens)
    dispatch(places_f, normed, send_f)
    exchange(1, send_f, got_f)
    mixing[...] = share(hits_f, places_f)[1]

    for load in loads[6:]:
        load.wait()
    arrive(0, send_b, got_b)
    widen(got_b)
    pick = onehot(
        iota((rows, rows), 1)
        == lax.rem(iota((rows, rows), 0), capacity) * devices
        + iota((rows, rows), 0) // capacity
    )

    def back_tile(number, inner):
        grad = dot_transposed(wide[...], down[columns(number), :])
        value = dot(pick, pre[:, columns(number)])
        gate = jax.nn.sigmoid(value)
        rounded = (value * gate).astype(jnp.bfloat16).astype(jnp.float32)
        mid[:, columns(number)] = (
            grad * gate * (1.0 + value * (1.0 - gate))
        ).astype(jnp.bfloat16)
        return inner + jnp.sum(grad * rounded, axis=1, keepdims=True)

    inner = lax.fori_loop(
        0, hidden_size // TILE, back_tile, jnp.zeros((rows, 1), jnp.float32)
    )
    spread = jnp.where(
        iota((rows, LANE), 1) == lax.rem(iota((rows, LANE), 0), capacity), inner, 0.0
    ).astype(jnp.bfloat16)
    gather = onehot(iota((devices, rows), 0) == iota((devices, rows), 1) // capacity)
    sums = dot(gather, spread)
    for number in range(devices):
        ret_s[number] = sums[number : number + 1, :]

    @pl.loop(0, width // TILE)
    def _(number):
        wide[:, columns(number)] = dot_transposed(
            mid[...], up[columns(number), :]
        ).astype(jnp.bfloat16)

    narrow(ret_b)
    exchange(4, ret_s, back_s)
    exchange(2, ret_b, back_b)

    arrive(1, send_f, got_f)
    widen(got_f)

    @pl.loop(0, hidden_size // TILE)
    def _(number):
        value = dot(wide[...], up[:, columns(number)])
        mid[:, columns(number)] = jax.nn.silu(value).astype(jnp.bfloat16)

    @pl.loop(0, width // TILE)
    def _(number):
        wide[:, columns(number)] = dot(mid[...], down[:, columns(number)]).astype(
            jnp.bfloat16
        )

    narrow(ret_f)
    exchange(3, ret_f, back_f)

    inv_rms = normalise(saved)
    shares_b, mixed_b = share(hits_b, places_b)
    arrive(4, ret_s, back_s)
    table = jnp.concatenate([back_s[number] for number in range(experts)], axis=0)
    totals = []
    for hit, rank in zip(hits_b, ranks_b):
        total = jnp.zeros((1, count), jnp.float32)
        for slot in range(capacity):
            named = jnp.sum(
                jnp.where(hit, table[:, slot : slot + 1], 0.0), axis=0, keepdims=True
            )
            total = total + jnp.where(rank == slot, named, 0.0)
        totals.append(total)
    whole = shares_b[0] * totals[0]
    for portion, total in zip(shares_b[1:], totals[1:]):
        whole = whole + portion * total
    logit_grad = jnp.zeros((experts, count), jnp.float32)
    for hit, portion, total in zip(hits_b, shares_b, totals):
        logit_grad = logit_grad + jnp.where(hit, portion * (total - whole), 0.0)
    logit_grad = dot_transposed(identity.astype(jnp.float32), logit_grad, HIGH)
    arrive(2, ret_b, back_b)
    widen(back_b)

    def grad_tile(number, total):
        grad = dot(mixed_b, wide[:, columns(number)]) + dot(
            logit_grad, router[:, columns(number)].astype(jnp.float32), HIGH
        )
        grad = grad * gain[:, columns(number)].astype(jnp.float32)
        gained[:, columns(number)] = grad
        value = saved[:, columns(number)].astype(jnp.float32)
        return total + jnp.sum(value * grad, axis=1, keepdims=True)

    total = lax.fori_loop(
        0, width // TILE, grad_tile, jnp.zeros((count, 1), jnp.float32)
    )
    along = inv_rms * inv_rms * inv_rms * (total / width)

    @pl.loop(0, width // TILE)
    def _(number):
        value = saved[:, columns(number)].astype(jnp.float32)
        grad = inv_rms * gained[:, columns(number)] - value * along
        out_b[:, columns(number)] = (
            upstream[:, columns(number)].astype(jnp.float32) + grad
        ).astype(jnp.bfloat16)

    arrive(3, ret_f, back_f)
    widen(back_f)

    @pl.loop(0, width // TILE)
    def _(number):
        value = tokens[:, columns(number)].astype(jnp.float32)
        out_f[:, columns(number)] = (
            value + dot(mixing[...], wide[:, columns(number)])
        ).astype(jnp.bfloat16)

    pass_back.wait_send()
    pass_on.wait_send()
    leave(0, send_b, got_b)
    leave(1, send_f, got_f)
    leave(2, ret_b, back_b)
    leave(3, ret_f, back_f)
    leave(4, ret_s, back_s)


def on_device(
    forward_sent,
    embedded,
    forward_routes,
    backward_sent,
    loss_gradient,
    saved_inputs,
    backward_routes,
    pre_activation,
    norm_gain,
    router,
    up_weight,
    down_weight,
):
    devices = lax.axis_size("expert")
    sections = lax.axis_size("section")
    experts = router.shape[2]
    capacity = pre_activation.shape[3]
    count, width = embedded.shape
    hidden_size = up_weight.shape[2]
    slots = experts * capacity
    saved_pre = pre_activation[0, :, 0].transpose(1, 0, 2).reshape(slots, hidden_size)
    vmem = pl.BlockSpec(memory_space=pltpu.VMEM)
    hbm = pl.BlockSpec(memory_space=pltpu.HBM)
    block = jax.ShapeDtypeStruct((count, width), jnp.bfloat16)
    held = pltpu.VMEM((count, width), jnp.bfloat16)
    lanes = pltpu.VMEM((slots * width // LANE, LANE), jnp.bfloat16)
    small = pltpu.VMEM((devices, 1, LANE), jnp.float32)
    forward_output, input_gradient = pl.pallas_call(
        functools.partial(relay_kernel, (devices, sections, experts, capacity)),
        out_shape=(block, block),
        in_specs=[hbm] * 12,
        out_specs=(vmem, vmem),
        scratch_shapes=[
            pltpu.VMEM(forward_routes.shape[:0:-1], jnp.int32),
            held,
            pltpu.VMEM(forward_routes.shape[:0:-1], jnp.int32),
            held,
            pltpu.VMEM((1, width), jnp.bfloat16),
            pltpu.VMEM((experts, width), jnp.bfloat16),
            pltpu.VMEM((hidden_size, width), jnp.bfloat16),
            pltpu.VMEM((slots, hidden_size), jnp.bfloat16),
            pltpu.VMEM((width, hidden_size), jnp.bfloat16),
            held,
            held,
            held,
            held,
            held,
            held,
            pltpu.VMEM((count, slots), jnp.bfloat16),
            pltpu.VMEM((count, width), jnp.float32),
            *[lanes] * 8,
            small,
            small,
            pltpu.VMEM((slots, width), jnp.bfloat16),
            pltpu.VMEM((slots, hidden_size), jnp.bfloat16),
            pltpu.SemaphoreType.DMA((10,)),
            pltpu.SemaphoreType.DMA((5, devices)),
            pltpu.SemaphoreType.DMA((5, devices)),
            pltpu.SemaphoreType.DMA((2,)),
            pltpu.SemaphoreType.DMA((2,)),
        ],
        compiler_params=pltpu.CompilerParams(
            collective_id=0, has_side_effects=True, vmem_limit_bytes=67_000_000
        ),
    )(
        forward_sent[0],
        backward_sent[0],
        backward_routes[0].T,
        loss_gradient,
        forward_routes[0].T,
        embedded,
        norm_gain,
        router[0].T,
        down_weight[0],
        saved_pre,
        up_weight[0],
        saved_inputs[0],
    )
    return (forward_output[None], input_gradient[None])


def solution(mesh):
    return jax.shard_map(
        on_device,
        mesh=mesh,
        in_specs=(
            P("section", "expert", None),
            P("expert", None),
            P("section", "expert", None),
            P("section", "expert", None),
            P("expert", None),
            P("section", "expert", None),
            P("section", "expert", None),
            P("section", None, "expert", None, None),
            P("section", None),
            P("section", None, None),
            P("expert", None, None),
            P("expert", None, None),
        ),
        out_specs=(P("section", "expert", None), P("section", "expert", None)),
        check_vma=False,
    )
```

time: 536 us -> 331 us (0.62)
  waiting for transfers between devices: 430 us -> 0 us
  Pallas kernels: 0 us -> 327 us
  starting transfers between devices: 59.6 us -> 0 us
  matrix products: 19.3 us -> 0 us
  local copies, waits for them, and re-layouts: 13.5 us -> 3.34 us
  other arithmetic: 6.81 us -> 0 us
    all_to_all x5 -> x0, waiting for transfers between devices: 430 us -> none  [the longest x1 105 us: on_device(): lax.all_to_all(result.reshape(sources, local_count * capacity, width), 'e...]
    pallas_call x0 -> x1, Pallas kernels: none -> 327 us  [on_device(): pl.pallas_call(functools.partial(relay_kernel, (devices, sections, expert...]
    all_to_all x5 -> x0, starting transfers between devices: 54.2 us -> none  [the longest x1 30 us: on_device(): lax.all_to_all(send_backward, 'expert', split_axis=0, concat_axis=0, tile...]
    dot_general x12 -> x0, matrix products: 19.3 us -> none  [the longest x1 5.76 us: on_device(): jnp.einsum('jecf,efd->jecd', hidden, down_weight, preferred_element_type=...]
    ppermute x2 -> x0, starting transfers between devices: 5.37 us -> none  [from_behind(): return lax.ppermute(block, axis, route)]
  transfers between devices with their start and end apart: 7 -> 0, of which waited for: 5 -> 0; matrix products, arithmetic and copies ran while one was open for 6% -> 0% of each run, Pallas kernels for 0% -> 0%
where the time goes in v2:
time: 331 us
  Pallas kernels  327 us (99%)
  local copies, waits for them, and re-layouts  3.34 us (1%)
    pallas_call x1, Pallas kernels, on_device(): pl.pallas_call(functools.partial(relay_kernel, (devices, sections, expert...  327 us

profile of v2, /device:TPU:1, one launch (start us, length us, event | category | flops | bytes accessed | tf_op | source)
XLA Modules:
  0.0 330.6 jit_solution(7963567571459228230)
XLA Ops:
  0.6 326.6 %shard_map.131 = (bf16[64,2048]{1,0:T(8,128)(2,1)}, bf16[64,2048]{1,0:T(8,128)(2,1)}) custom-call(bf16[64,2048]{1,0:T(8,128)(2,1)} %bitcast.24, bf16[64,2048]{1,0:T(8,128)(2,1)} %bitcast.25, s32[2,64]{1,0:T(2,128)} %bitcast.30, bf16[64,2048]{1,0:T(8,128)(2,1)} %loss_hbm.1, s32[2,64]{1,0:T(2,128)} %bitcast.31, bf16[64,2048]{1,0:T(8,128)(2,1)} %embedded_hbm.1, ...), custom_call_target="tpu_custom_call" | custom-call | tf_op jit(solution)/shard_map/pallas_call | solution.py:479
  327.3 1.7 copy.16
  328.9 1.7 copy.17

commit v3 on v2

--- a/solution.py
+++ b/solution.py
@@ -179,15 +179,15 @@
 
     def arrive(stage, source, target):
         for_peers(
-            lambda number, peer: copy_of(
-                stage, number, peer, source, target
+            lambda number, _: copy_of(
+                stage, number, partner, source, target
             ).wait_recv()
         )
 
     def leave(stage, source, target):
         for_peers(
-            lambda number, peer: copy_of(
-                stage, number, peer, source, target
+            lambda number, _: copy_of(
+                stage, number, partner, source, target
             ).wait_send()
         )
 
@@ -384,6 +384,10 @@
     narrow(ret_f)
     exchange(3, ret_f, back_f)
 
+    pass_back.wait_send()
+    pass_on.wait_send()
+    leave(0, send_b, got_b)
+    leave(1, send_f, got_f)
     inv_rms = normalise(saved)
     shares_b, mixed_b = share(hits_b, places_b)
     arrive(4, ret_s, back_s)
@@ -429,6 +433,8 @@
             upstream[:, columns(number)].astype(jnp.float32) + grad
         ).astype(jnp.bfloat16)
 
+    leave(4, ret_s, back_s)
+    leave(2, ret_b, back_b)
     arrive(3, ret_f, back_f)
     widen(back_f)
 
@@ -439,13 +445,7 @@
             value + dot(mixing[...], wide[:, columns(number)])
         ).astype(jnp.bfloat16)
 
-    pass_back.wait_send()
-    pass_on.wait_send()
-    leave(0, send_b, got_b)
-    leave(1, send_f, got_f)
-    leave(2, ret_b, back_b)
     leave(3, ret_f, back_f)
-    leave(4, ret_s, back_s)
 
 
 def on_device(

time: 331 us -> 329 us (level)
  no operation moved by 1% of the time
where the time goes in v3:
time: 329 us
  Pallas kernels  325 us (99%)
  local copies, waits for them, and re-layouts  3.34 us (1%)
    pallas_call x1, Pallas kernels, on_device(): pl.pallas_call(functools.partial(relay_kernel, (devices, sections, expert...  325 us

profile of v3, /device:TPU:1, one launch (start us, length us, event | category | flops | bytes accessed | tf_op | source)
XLA Modules:
  0.0 328.9 jit_solution(9285833875764877831)
XLA Ops:
  0.6 324.9 %shard_map.131 = (bf16[64,2048]{1,0:T(8,128)(2,1)}, bf16[64,2048]{1,0:T(8,128)(2,1)}) custom-call(bf16[64,2048]{1,0:T(8,128)(2,1)} %bitcast.24, bf16[64,2048]{1,0:T(8,128)(2,1)} %bitcast.25, s32[2,64]{1,0:T(2,128)} %bitcast.30, bf16[64,2048]{1,0:T(8,128)(2,1)} %loss_hbm.1, s32[2,64]{1,0:T(2,128)} %bitcast.31, bf16[64,2048]{1,0:T(8,128)(2,1)} %embedded_hbm.1, ...), custom_call_target="tpu_custom_call" | custom-call | tf_op jit(solution)/shard_map/pallas_call | solution.py:479
  325.6 1.7 copy.16
  327.2 1.7 copy.17
